TPU v7x, 32 devices: a whole 2x2x4 slice. The times are simulated.
32 devices in a mesh: fsdp: 8 (over z, y), tp: 4 (over x, core).
Axes of the slice: x: 2, y: 2, z: 4, core: 2. Of those that a mesh axis runs over, the one named last changes fastest.
Arguments:
- grads: bfloat16 [8, 2, 4096, 2048], P('fsdp', None, 'tp'), may hold values from -144 to 144
- master: float32 [4096, 2048], P('tp', 'fsdp'), may hold values from -0.3125 to 0.3125
- moment: float32 [4096, 2048], P('tp', 'fsdp'), may hold values from -1.5 to 1.5
- second: float32 [4096, 2048], P('tp', 'fsdp'), may hold values from 0.02 to 0.3
- stats: float32 [4, 1024, 1024], P('tp', 'fsdp'), may hold values from -0.05 to 0.35
- basis: float32 [4, 1024, 1024], P('tp', 'fsdp'), may hold values from -0.5 to 1.5
Outputs:
- weights: bfloat16 [4096, 2048], P('tp')
- master_new: float32 [4096, 2048], P('tp', 'fsdp')
- moment_new: float32 [4096, 2048], P('tp', 'fsdp')
- second_new: float32 [4096, 2048], P('tp', 'fsdp')
- stats_new: float32 [4, 1024, 1024], P('tp', 'fsdp')
- basis_new: float32 [4, 1024, 1024], P('tp', 'fsdp')
All inputs are finite; a program needn't handle non-finite values.
Results may differ from a plain program's by a relative error of at most 0.007.
Values may be sent and summed in bfloat16 or wider, within the bound.
A program may use at most 128 MiB of HBM per device.

v0:
```python
import jax
import jax.numpy as jnp
from jax import lax
from jax.sharding import PartitionSpec as P

D = 4096
KVW = 2048
NSK = 2
poly_first = 3.4445
poly_second = -4.775
poly_third = 2.0315


def gram_of(current):
    local_gram = jnp.dot(current.T, current, precision=lax.Precision.HIGHEST)
    return lax.psum(local_gram.astype(jnp.bfloat16), "fsdp").astype(jnp.float32)


def body(grads, master, moment, second, stats, basis):
    high = lax.Precision.HIGHEST
    local = jnp.sum(grads.astype(jnp.float32), axis=(0, 1))
    summed = lax.psum_scatter(local, "fsdp", scatter_dimension=1, tiled=True)
    squares = lax.psum(jnp.sum(summed * summed), ("fsdp", "tp"))
    clipped = summed * jnp.minimum(1.0, jnp.sqrt(float(D * KVW) / (squares + 1e-06)))
    own_rows = basis[0]
    stat_rows = stats[0]
    whole = lax.all_gather(own_rows, "fsdp", axis=0, tiled=True)
    rotated = jnp.dot(whole.T, clipped, precision=high)
    moment_new = 0.9 * moment + 0.1 * rotated
    second_new = 0.95 * second + 0.05 * rotated * rotated
    update = moment_new / (jnp.sqrt(second_new) + 1e-08)
    delta = jnp.dot(whole, update, precision=high)
    master_new = master - 0.01 * (delta + 0.1 * master)
    weights = lax.all_gather(master_new.astype(jnp.bfloat16), "fsdp", axis=1, tiled=True)
    outer = lax.psum_scatter(
        jnp.dot(clipped, clipped.T, precision=high).astype(jnp.bfloat16),
        "fsdp",
        scatter_dimension=0,
        tiled=True,
    ).astype(jnp.float32)
    stats_new = 0.9 * stat_rows + 0.1 / KVW * outer
    power = jnp.dot(stats_new, whole, precision=high)
    total_sq = lax.psum(jnp.sum(power * power), "fsdp")
    current = power / jnp.sqrt(total_sq + 1e-06)
    first_gram = gram_of(current)
    for step in range(NSK):
        gram = first_gram if step == 0 else gram_of(current)
        product = jnp.dot(current, gram, precision=high)
        second_term = jnp.dot(product, gram, precision=high)
        current = poly_first * current + poly_second * product + poly_third * second_term
    return (weights, master_new, moment_new, second_new, stats_new[None], current[None])


def solution(mesh):
    in_specs = (
        P("fsdp", None, "tp", None),
        P("tp", "fsdp"),
        P("tp", "fsdp"),
        P("tp", "fsdp"),
        P("tp", "fsdp", None),
        P("tp", "fsdp", None),
    )
    out_specs = (
        P("tp", None),
        P("tp", "fsdp"),
        P("tp", "fsdp"),
        P("tp", "fsdp"),
        P("tp", "fsdp", None),
        P("tp", "fsdp", None),
    )
    return jax.shard_map(body, mesh=mesh, in_specs=in_specs, out_specs=out_specs, check_vma=False)
```

profile of v0, /device:TPU:0, one launch (start us, length us, event | category | flops | bytes accessed | tf_op | source)
XLA Modules:
  0.0 637.1 jit_solution(12777365153382909776)
XLA Ops:
  7.2 9.6 %convert_reduce_fusion = f32[1024,2048]{1,0:T(8,128)} fusion(bf16[1,2,1024,2048]{3,2,1,0:T(8,128)(2,1)} %param.6), kind=kLoop, calls=%fused_computation | loop fusion | flops 6291456 | bytes 16777216 | tf_op jit(solution)/shard_map/reduce_sum | solution.py:21
  16.9 0.7 all-gather.6.cloned.1.call-update
  17.6 151.5 %reduce-scatter.3.cloned.1.call-done = f32[1024,256]{1,0:T(8,128)} async-done(((f32[1024,2048]{1,0:T(8,128)}), f32[1024,256]{1,0:T(8,128)}) %reduce-scatter.3.cloned.1.call-update) | async-done | bytes 1048592 | tf_op jit(solution)/shard_map/reduce_scatter | solution.py:22
  169.1 2.1 multiply_reduce_fusion
  171.2 40.6 %psum.28 = f32[]{:T(128)} all-reduce(f32[]{:T(128)} %multiply_reduce_fusion), channel_id=1, replica_groups=mesh['fsdp'=8,'tp'=4] {'fsdp','tp'}, use_global_device_ids=true, to_apply=%region_3.0 | all-reduce | flops 1 | bytes 8 | tf_op jit(solution)/shard_map/psum | solution.py:23
  212.6 6.4 %convolution_convert_fusion.2 = bf16[1024,1024]{1,0:T(8,128)(2,1)} fusion(f32[1024,256]{1,0:T(8,128)} %reduce-scatter.3.cloned.1.call-done, f32[]{:T(128)S(6)} %min_shard_map.3), kind=kOutput, calls=%fused_computation.9 | convolution fusion | flops 3222536192 | bytes 3145732 | tf_op jit(solution)/shard_map/dot_general | solution.py:36
  219.0 0.0 all-reduce.3.cloned.1.call-start
  219.1 26.4 %all-gather.6.cloned.1.call-done = f32[1,1024,1024]{2,1,0:T(8,128)} async-done(((f32[1,128,1024]{2,1,0:T(8,128)}), f32[1,1024,1024]{2,1,0:T(8,128)}) %all-gather.6.cloned.1.call-update) | async-done | bytes 4194320 | tf_op jit(solution)/shard_map/all_gather | solution.py:27
  245.4 70.4 %reduce-scatter.5.cloned.1.call-done = bf16[128,1024]{1,0:T(8,128)(2,1)} async-done(((bf16[1024,1024]{1,0:T(8,128)(2,1)}), bf16[128,1024]{1,0:T(8,128)(2,1)}) %reduce-scatter.5.cloned.1.call-update) | async-done | bytes 262160 | tf_op jit(solution)/shard_map/reduce_scatter | solution.py:35
  315.8 5.3 multiply_reduce_fusion.1
  321.2 19.9 %psum.29 = f32[]{:T(128)} all-reduce(f32[]{:T(128)} %get-tuple-element.22), channel_id=1, replica_groups=mesh['fsdp'=8,'tp'=4] {'fsdp'}, use_global_device_ids=true, to_apply=%region_6.0 | all-reduce | flops 1 | bytes 8 | tf_op jit(solution)/shard_map/psum | solution.py:43
  341.8 4.7 convolution_convert_fusion.1
  346.5 0.0 all-gather.4.cloned.1.call-start
  346.6 1.3 copy.20
  347.9 2.5 copy.21
  350.4 2.5 copy.23
  352.9 6.7 %fusion.24 = (f32[1024,256]{0,1:T(8,128)S(1)}, f32[1024,256]{0,1:T(8,128)S(1)}) fusion(f32[1024,256]{0,1:T(8,128)} %copy.21, f32[1024,256]{0,1:T(8,128)} %copy.20, f32[1,1024,1024]{2,1,0:T(8,128)} %all-gather.6.cloned.1.call-done, f32[1024,256]{1,0:T(8,128)S(1)} %copy-done.1, f32[]{:T(128)S(6)} %min_shard_map.3), kind=kOutput, calls=%fused_computation.21 | convolution fusion | flops 3223322624 | bytes 9437188 | tf_op jit(solution)/shard_map/dot_general | solution.py:28
  359.6 5.3 fusion.40
  364.9 0.3 all-reduce.5.cloned.1.call-start
  365.2 80.5 %all-reduce.3.cloned.1.call-done = bf16[1024,1024]{1,0:T(8,128)(2,1)} async-done(((bf16[1024,1024]{1,0:T(8,128)(2,1)}), bf16[1024,1024]{1,0:T(8,128)(2,1)}) %all-reduce.3.cloned.1.call-update) | async-done | bytes 2097168 | tf_op jit(solution)/shard_map/psum | solution.py:16
  445.7 2.6 fusion.39
  448.4 2.6 fusion.23
  451.0 4.7 convolution_convert_fusion
  455.8 1.3 copy.26
  457.1 1.3 copy.27
  458.4 2.5 copy.25
  460.9 0.9 fusion.33
  461.8 59.9 %all-gather.4.cloned.1.call-done = bf16[1024,2048]{0,1:T(8,128)(2,1)} async-done(((bf16[1024,256]{0,1:T(8,128)(2,1)}), bf16[1024,2048]{0,1:T(8,128)(2,1)}) %all-gather.4.cloned.1.call-update) | async-done | bytes 4194320 | tf_op jit(solution)/shard_map/all_gather | solution.py:34
  521.7 6.4 %copy.24 = bf16[1024,2048]{1,0:T(8,128)(2,1)} copy(bf16[1024,2048]{0,1:T(8,128)(2,1)} %all-gather.4.cloned.1.call-done) | data formatting | bytes 8388608
  528.1 97.6 %all-reduce.5.cloned.1.call-done = bf16[1024,1024]{1,0:T(8,128)(2,1)} async-done(((bf16[1024,1024]{1,0:T(8,128)(2,1)}), bf16[1024,1024]{1,0:T(8,128)(2,1)}) %all-reduce.5.cloned.1.call-update) | async-done | bytes 2097168 | tf_op jit(solution)/shard_map/psum | solution.py:16
  625.7 2.8 fusion.41
  628.4 1.9 fusion.22
  (28 shorter events, 0.2 us)
Async XLA Ops:
  7.2 161.9 %reduce-scatter.3.cloned.1.call-start = ((), (), s32[]{:S(2)}) async-start(), calls=%async_computation.2 | async-start | bytes 9437184 | tf_op jit(solution)/shard_map/reduce_scatter | solution.py:22
  16.8 299.0 %copy-start.4 = (f32[1,128,1024]{2,1,0:T(8,128)S(1)}, f32[1,128,1024]{2,1,0:T(8,128)}, u32[]{:S(2)}) copy-start(f32[1,128,1024]{2,1,0:T(8,128)} %param.10) | copy-start | bytes 1572868
  16.8 228.6 %all-gather.6.cloned.1.call-start = ((), (), s32[]{:S(2)}) async-start(), calls=%async_computation.7 | async-start | bytes 4718592 | tf_op jit(solution)/shard_map/all_gather | solution.py:27
  17.6 298.2 %reduce-scatter.5.cloned.1.call-start = ((), (), s32[]{:S(2)}) async-start(), calls=%async_computation.4 | async-start | bytes 2359296 | tf_op jit(solution)/shard_map/reduce_scatter | solution.py:35
  219.0 127.5 %copy-start.9 = (f32[1024,256]{1,0:T(8,128)S(1)}, f32[1024,256]{1,0:T(8,128)}, u32[]{:S(2)}) copy-start(f32[1024,256]{1,0:T(8,128)} %param.8) | copy-start | bytes 3145732
  219.0 226.7 %all-reduce.3.cloned.1.call-start = ((), (), s32[]{:S(2)}) async-start(), calls=%async_computation.5 | async-start | bytes 4194304 | tf_op jit(solution)/shard_map/psum | solution.py:16
  321.2 29.2 %copy-start.6 = (f32[128,1024]{1,0:T(8,128)}, f32[128,1024]{1,0:T(8,128)S(1)}, u32[]{:S(2)}) copy-start(f32[128,1024]{1,0:T(8,128)S(1)} %get-tuple-element.23) | copy-start | bytes 1572868
  346.5 6.5 %copy-start.1 = (f32[1024,256]{1,0:T(8,128)S(1)}, f32[1024,256]{1,0:T(8,128)}, u32[]{:S(2)}) copy-start(f32[1024,256]{1,0:T(8,128)} %reduce-scatter.3.cloned.1.call-done) | copy-start | bytes 3145732
  346.5 175.2 %all-gather.4.cloned.1.call-start = ((), (), s32[]{:S(2)}) async-start(), calls=%async_computation.3 | async-start | bytes 4718592 | tf_op jit(solution)/shard_map/all_gather | solution.py:34
  352.9 6.7 %copy-start = (f32[1,1024,1024]{2,1,0:T(8,128)S(1)}, f32[1,1024,1024]{2,1,0:T(8,128)}, u32[]{:S(2)}) copy-start(f32[1,1024,1024]{2,1,0:T(8,128)} %all-gather.6.cloned.1.call-done) | copy-start | bytes 12582916
  352.9 6.7 %copy-start.3 = (f32[1024,256]{0,1:T(8,128)S(1)}, f32[1024,256]{0,1:T(8,128)}, u32[]{:S(2)}) copy-start(f32[1024,256]{0,1:T(8,128)} %copy.23) | copy-start | bytes 3145732
  359.6 86.1 %copy-start.7 = (f32[128,1024]{1,0:T(8,128)S(1)}, f32[128,1024]{1,0:T(8,128)}, u32[]{:S(2)}) copy-start(f32[128,1024]{1,0:T(8,128)} %copy-done.6) | copy-start | bytes 1572868
  364.9 260.7 %all-reduce.5.cloned.1.call-start = ((), (), s32[]{:S(2)}) async-start(), calls=%async_computation.6 | async-start | bytes 4194304 | tf_op jit(solution)/shard_map/psum | solution.py:16
  455.7 5.2 copy-start.5
  455.7 5.2 copy-start.8
  625.7 2.8 copy-start.2
Sparse Core Ops, SparseCore 0:
  16.9 152.0 reduce-scatter.2
  171.4 73.9 all-gather.5
  250.0 65.8 reduce-scatter.4
  346.6 99.0 all-reduce.2
  448.5 73.1 all-gather.3
  525.6 100.0 all-reduce.4
where the time goes:
time: 638 us; the launch traced here: 637 us
  waiting for transfers between devices  487 us (76%)
  blocking collectives  60.5 us (9%)
  matrix products  43 us (7%)
  local copies, waits for them, and re-layouts  18 us (3%)
  between operations  15.6 us (2%)
  other arithmetic  12.6 us (2%)
    psum x2, waiting for transfers between devices, gram_of(): return lax.psum(local_gram.astype(jnp.bfloat16), 'fsdp').astype(jnp.float32)  178 us
    reduce_scatter x1, waiting for transfers between devices, body(): summed = lax.psum_scatter(local, 'fsdp', scatter_dimension=1, tiled=True)  151 us
    reduce_scatter x1, waiting for transfers between devices, body(): lax.psum_scatter(jnp.dot(clipped, clipped.T, precision=high).astype(jnp.b...  70.4 us
    all_gather x1, waiting for transfers between devices, body(): lax.all_gather(master_new.astype(jnp.bfloat16), 'fsdp', axis=1, tiled=True)  59.9 us
    psum x1, blocking collectives, body(): squares = lax.psum(jnp.sum(summed * summed), ('fsdp', 'tp'))  40.6 us
    all_gather x1, waiting for transfers between devices, body(): whole = lax.all_gather(own_rows, 'fsdp', axis=0, tiled=True)  26.4 us
    psum x1, blocking collectives, body(): total_sq = lax.psum(jnp.sum(power * power), 'fsdp')  19.9 us
    unnamed x27, local copies, waits for them, and re-layouts  18 us
  transfers between devices with their start and end apart: 6, of which 6 were waited for; matrix products, arithmetic and copies ran while one was open for 8% of the time, Pallas kernels for 0%

commit v1 on v0

--- a/solution.py
+++ b/solution.py
@@ -13,7 +13,9 @@
 
 def gram_of(current):
     local_gram = jnp.dot(current.T, current, precision=lax.Precision.HIGHEST)
-    return lax.psum(local_gram.astype(jnp.bfloat16), "fsdp").astype(jnp.float32)
+    return jnp.sum(lax.all_gather(local_gram.astype(jnp.bfloat16), "fsdp"), axis=0).astype(
+        jnp.float32
+    )
 
 
 def body(grads, master, moment, second, stats, basis):

time: 638 us -> 894 us (1.40)
  waiting for transfers between devices: 487 us -> 724 us
  other arithmetic: 12.6 us -> 32.9 us
    all_gather x0 -> x2, waiting for transfers between devices: none -> 427 us  [gram_of(): lax.all_gather(local_gram.astype(jnp.bfloat16), 'fsdp')]
    psum x2 -> x0, waiting for transfers between devices: 178 us -> none  [gram_of(): return lax.psum(local_gram.astype(jnp.bfloat16), 'fsdp').astype(jnp.float32)]
    reduce_sum x0 -> x2, other arithmetic: none -> 20.4 us  [gram_of(): jnp.sum(lax.all_gather(local_gram.astype(jnp.bfloat16), 'fsdp'), axis=0)]
    all_gather x1, waiting for transfers between devices: 59.9 us -> 47.3 us  [body(): lax.all_gather(master_new.astype(jnp.bfloat16), 'fsdp', axis=1, tiled=True)]
    unnamed x27 -> x25, local copies, waits for them, and re-layouts: 18 us -> 18.2 us
  transfers between devices with their start and end apart: 6 -> 6, of which waited for: 6 -> 6; matrix products, arithmetic and copies ran while one was open for 8% -> 7% of each run, Pallas kernels for 0% -> 0%
where the time goes in v1:
time: 894 us
  waiting for transfers between devices  724 us (81%)
  blocking collectives  60.6 us (7%)
  matrix products  42.2 us (5%)
  other arithmetic  32.9 us (4%)
  local copies, waits for them, and re-layouts  18.2 us (2%)
  between operations  15.6 us (2%)
    all_gather x2, waiting for transfers between devices, gram_of(): lax.all_gather(local_gram.astype(jnp.bfloat16), 'fsdp')  427 us
    reduce_scatter x1, waiting for transfers between devices, body(): summed = lax.psum_scatter(local, 'fsdp', scatter_dimension=1, tiled=True)  151 us
    reduce_scatter x1, waiting for transfers between devices, body(): lax.psum_scatter(jnp.dot(clipped, clipped.T, precision=high).astype(jnp.b...  70.7 us
    all_gather x1, waiting for transfers between devices, body(): lax.all_gather(master_new.astype(jnp.bfloat16), 'fsdp', axis=1, tiled=True)  47.3 us
    psum x1, blocking collectives, body(): squares = lax.psum(jnp.sum(summed * summed), ('fsdp', 'tp'))  40.6 us
    all_gather x1, waiting for transfers between devices, body(): whole = lax.all_gather(own_rows, 'fsdp', axis=0, tiled=True)  26.5 us
    reduce_sum x2, other arithmetic, gram_of(): jnp.sum(lax.all_gather(local_gram.astype(jnp.bfloat16), 'fsdp'), axis=0)  20.4 us
    psum x1, blocking collectives, body(): total_sq = lax.psum(jnp.sum(power * power), 'fsdp')  20 us
  transfers between devices with their start and end apart: 6, of which 6 were waited for; matrix products, arithmetic and copies ran while one was open for 7% of the time, Pallas kernels for 0%

profile of v1, /device:TPU:0, one launch (start us, length us, event | category | flops | bytes accessed | tf_op | source)
XLA Modules:
  0.0 893.6 jit_solution(2117042240737282096)
XLA Ops:
  7.2 9.6 %convert_reduce_fusion = f32[1024,2048]{1,0:T(8,128)} fusion(bf16[1,2,1024,2048]{3,2,1,0:T(8,128)(2,1)} %param.6), kind=kLoop, calls=%fused_computation | loop fusion | flops 6291456 | bytes 16777216 | tf_op jit(solution)/shard_map/reduce_sum | solution.py:23
  16.9 0.7 all-gather.10.cloned.1.call-update
  17.6 151.5 %reduce-scatter.3.cloned.1.call-done = f32[1024,256]{1,0:T(8,128)} async-done(((f32[1024,2048]{1,0:T(8,128)}), f32[1024,256]{1,0:T(8,128)}) %reduce-scatter.3.cloned.1.call-update) | async-done | bytes 1048592 | tf_op jit(solution)/shard_map/reduce_scatter | solution.py:24
  169.1 2.1 multiply_reduce_fusion
  171.2 40.6 %psum.14 = f32[]{:T(128)} all-reduce(f32[]{:T(128)} %multiply_reduce_fusion), channel_id=1, replica_groups=mesh['fsdp'=8,'tp'=4] {'fsdp','tp'}, use_global_device_ids=true, to_apply=%region_3.0 | all-reduce | flops 1 | bytes 8 | tf_op jit(solution)/shard_map/psum | solution.py:25
  212.5 6.4 convolution_convert_fusion.2
  219.0 26.5 %all-gather.10.cloned.1.call-done = f32[1,1024,1024]{2,1,0:T(8,128)} async-done(((f32[1,128,1024]{2,1,0:T(8,128)}), f32[1,1024,1024]{2,1,0:T(8,128)}) %all-gather.10.cloned.1.call-update) | async-done | bytes 4194320 | tf_op jit(solution)/shard_map/all_gather | solution.py:29
  245.4 70.7 %reduce-scatter.5.cloned.1.call-done = bf16[128,1024]{1,0:T(8,128)(2,1)} async-done(((bf16[1024,1024]{1,0:T(8,128)(2,1)}), bf16[128,1024]{1,0:T(8,128)(2,1)}) %reduce-scatter.5.cloned.1.call-update) | async-done | bytes 262160 | tf_op jit(solution)/shard_map/reduce_scatter | solution.py:37
  316.1 5.3 multiply_reduce_fusion.1
  321.5 20.0 %psum.15 = f32[]{:T(128)} all-reduce(f32[]{:T(128)} %get-tuple-element.22), channel_id=1, replica_groups=mesh['fsdp'=8,'tp'=4] {'fsdp'}, use_global_device_ids=true, to_apply=%region_6.0 | all-reduce | flops 1 | bytes 8 | tf_op jit(solution)/shard_map/psum | solution.py:45
  342.1 4.7 convolution_convert_fusion.1
  346.9 1.3 copy.20
  348.2 2.5 copy.21
  350.8 2.7 copy.23
  353.5 7.5 fusion.24
  361.0 5.3 fusion.40
  366.3 0.3 all-gather.14.cloned.1.call-start
  366.6 205.3 %all-gather.12.cloned.1.call-done = bf16[8192,1024]{1,0:T(8,128)(2,1)} async-done(((bf16[1024,1024]{1,0:T(8,128)(2,1)}), bf16[8192,1024]{1,0:T(8,128)(2,1)}) %all-gather.12.cloned.1.call-update) | async-done | bytes 16777232 | tf_op jit(solution)/shard_map/all_gather | solution.py:16
  571.9 10.9 %reduce_sum.54 = bf16[1024,1024]{1,0:T(8,128)(2,1)} reduce(bf16[8,1024,1024]{2,1,0:T(8,128)(2,1)} %bitcast.55, bf16[]{:T(256)} %constant.14.clone.1), dimensions={0}, to_apply=%region_7.0 | reduce | flops 7340032 | bytes 18874370 | tf_op jit(solution)/shard_map/reduce_sum | solution.py:16
  582.8 2.6 fusion.39
  585.4 2.7 fusion.23
  588.1 4.8 convolution_convert_fusion
  592.9 1.3 copy.26
  594.2 1.3 copy.27
  595.5 2.5 copy.25
  598.1 0.9 fusion.33
  598.9 47.3 %all-gather.8.cloned.1.call-done = bf16[1024,2048]{0,1:T(8,128)(2,1)} async-done(((bf16[1024,256]{0,1:T(8,128)(2,1)}), bf16[1024,2048]{0,1:T(8,128)(2,1)}) %all-gather.8.cloned.1.call-update) | async-done | bytes 4194320 | tf_op jit(solution)/shard_map/all_gather | solution.py:36
  646.3 6.4 copy.24
  652.7 221.7 %all-gather.14.cloned.1.call-done = bf16[8192,1024]{1,0:T(8,128)(2,1)} async-done(((bf16[1024,1024]{1,0:T(8,128)(2,1)}), bf16[8192,1024]{1,0:T(8,128)(2,1)}) %all-gather.14.cloned.1.call-update) | async-done | bytes 16777232 | tf_op jit(solution)/shard_map/all_gather | solution.py:16
  874.4 9.5 %reduce_sum.55 = bf16[1024,1024]{1,0:T(8,128)(2,1)S(1)} reduce(bf16[8,1024,1024]{2,1,0:T(8,128)(2,1)} %bitcast.56, bf16[]{:T(256)} %constant.14.clone.1), dimensions={0}, to_apply=%region_8.0 | reduce | flops 7340032 | bytes 18874370 | tf_op jit(solution)/shard_map/reduce_sum | solution.py:16
  883.8 1.0 fusion.41
  884.9 1.9 fusion.22
  (28 shorter events, 0.3 us)
Async XLA Ops:
  7.2 161.9 %reduce-scatter.3.cloned.1.call-start = ((), (), s32[]{:S(2)}) async-start(), calls=%async_computation.2 | async-start | bytes 9437184 | tf_op jit(solution)/shard_map/reduce_scatter | solution.py:24
  16.8 299.3 %copy-start.3 = (f32[1,128,1024]{2,1,0:T(8,128)S(1)}, f32[1,128,1024]{2,1,0:T(8,128)}, u32[]{:S(2)}) copy-start(f32[1,128,1024]{2,1,0:T(8,128)} %param.10) | copy-start | bytes 1572868
  16.8 228.6 %all-gather.10.cloned.1.call-start = ((), (), s32[]{:S(2)}) async-start(), calls=%async_computation.5 | async-start | bytes 4718592 | tf_op jit(solution)/shard_map/all_gather | solution.py:29
  17.6 298.6 %reduce-scatter.5.cloned.1.call-start = ((), (), s32[]{:S(2)}) async-start(), calls=%async_computation.4 | async-start | bytes 2359296 | tf_op jit(solution)/shard_map/reduce_scatter | solution.py:37
  218.9 128.0 %copy-start.8 = (f32[1024,256]{1,0:T(8,128)S(1)}, f32[1024,256]{1,0:T(8,128)}, u32[]{:S(2)}) copy-start(f32[1024,256]{1,0:T(8,128)} %param.8) | copy-start | bytes 3145732
  218.9 352.9 %all-gather.12.cloned.1.call-start = ((), (), s32[]{:S(2)}) async-start(), calls=%async_computation.6 | async-start | bytes 18874368 | tf_op jit(solution)/shard_map/all_gather | solution.py:16
  321.5 29.3 %copy-start.5 = (f32[128,1024]{1,0:T(8,128)}, f32[128,1024]{1,0:T(8,128)S(1)}, u32[]{:S(2)}) copy-start(f32[128,1024]{1,0:T(8,128)S(1)} %get-tuple-element.23) | copy-start | bytes 1572868
  346.8 6.6 copy-start.1
  346.9 299.4 %all-gather.8.cloned.1.call-start = ((), (), s32[]{:S(2)}) async-start(), calls=%async_computation.3 | async-start | bytes 4718592 | tf_op jit(solution)/shard_map/all_gather | solution.py:36
  353.5 7.5 copy-start
  353.5 7.6 copy-start.2
  366.3 508.0 %all-gather.14.cloned.1.call-start = ((), (), s32[]{:S(2)}) async-start(), calls=%async_computation.7 | async-start | bytes 18874368 | tf_op jit(solution)/shard_map/all_gather | solution.py:16
  571.9 10.9 %copy-start.6 = (f32[128,1024]{1,0:T(8,128)S(1)}, f32[128,1024]{1,0:T(8,128)}, u32[]{:S(2)}) copy-start(f32[128,1024]{1,0:T(8,128)} %copy-done.5) | copy-start | bytes 1572868
  592.9 5.2 copy-start.4
  592.9 5.2 copy-start.7
Sparse Core Ops, SparseCore 0:
  16.9 152.0 reduce-scatter.2
  171.4 73.9 all-gather.9
  250.0 66.1 reduce-scatter.4
  347.0 224.8 all-gather.11
  574.6 71.5 all-gather.7
  648.5 225.8 all-gather.13
